TPU v7x, 32 devices: a whole 2x2x4 slice. The times are simulated.
32 devices in a mesh: ctx: 4 (over y, x), head: 8 (over z, core).
Axes of the slice: x: 2, y: 2, z: 4, core: 2. Of those that a mesh axis runs over, the one named last changes fastest.
Arguments:
- queries: bfloat16 [4096, 8192], P('ctx', 'head'), may hold values from -12 to 12
- key_heads: bfloat16 [1024, 4096], P(None, 'ctx'), may hold values from -6 to 6
- value_heads: bfloat16 [1024, 4096], P(None, 'ctx'), may hold values from -6 to 6
- out_weight: bfloat16 [8192, 8192], P('head'), may hold values from -0.09375 to 0.09375
- block_order: int32 [8], replicated, may hold values from 0 to 7, each once
- doc_ids: int32 [4096], replicated, may hold values from 0 to 5, never falling along the last dimension, each value on 1 to 1024 neighbouring positions
Outputs:
- projected: bfloat16 [4096, 8192], P('ctx', 'head')
Inputs may be any that keep to these rules, and one draw needn't show every extreme that they name: Layout slot j (rows j * 512 to (j + 1) * 512 - 1 of queries and projected, the same columns of key_heads and value_heads) holds block block_order[j] of the sequence; each of 0 to 7 appears once. `doc_ids`: ids never fall along the sequence; every id is used; each document holds 1 to 1024 tokens and one holds exactly 1024.
All inputs are finite; a program needn't handle non-finite values.
Results may differ from a plain program's by a relative error of at most 0.014.
Values may be sent and summed in bfloat16 or wider, within the bound.
No kernel may reach another device: no remote copies, remote signals or barrier semaphores. Data moves between devices by JAX's collectives and lax.ppermute only.
A program may use at most 192 MiB of HBM per device.

v0:
```python
import jax
import jax.numpy as jnp
from jax import lax
from jax.sharding import PartitionSpec as P

KVH = 8
HD = 128
floor_score = -1e30


def locate(row_ids, block_order, doc_ids):
    block_len = doc_ids.shape[0] // block_order.shape[0]
    block_id = row_ids // block_len
    slot_table = jnp.arange(block_order.shape[0], dtype=jnp.int32)
    starts = jnp.sum(
        jnp.where(block_id[:, None] == slot_table[None, :], block_order[None, :], 0), axis=1
    )
    places = starts * block_len + row_ids % block_len
    return (places, jnp.take(doc_ids, places))


def attend_block(
    running, key_block, value_block, key_place, key_doc, query_heads, query_place, query_doc
):
    visible = (key_place[None, :] <= query_place[:, None]) & (
        key_doc[None, :] == query_doc[:, None]
    )
    row_top, row_total, row_accum = running
    scores = jnp.einsum(
        "thd,dk->thk", query_heads, key_block, preferred_element_type=jnp.float32
    ) * key_block.shape[0] ** (-0.5)
    scores = jnp.where(visible[:, None, :], scores, floor_score)
    new_top = jnp.maximum(row_top, jnp.max(scores, axis=2))
    factor = jnp.exp(row_top - new_top)
    weights = jnp.where(visible[:, None, :], jnp.exp(scores - new_top[:, :, None]), 0.0)
    row_total = row_total * factor + jnp.sum(weights, axis=2)
    mixed = jnp.einsum(
        "thk,dk->thd", weights.astype(jnp.bfloat16), value_block, preferred_element_type=jnp.float32
    )
    row_accum = row_accum * factor[:, :, None] + mixed
    return (new_top, row_total, row_accum)


def attend_span(
    running, key_piece, value_piece, query_heads, query_place, query_doc, block_order, doc_ids
):
    key_count = key_piece.shape[1]
    block_width = 1024
    rounds = key_count // block_width
    places, doc_list = locate(jnp.arange(key_count, dtype=jnp.int32), block_order, doc_ids)

    def one_round(round_index, current):
        offset = round_index * block_width
        return attend_block(
            current,
            lax.dynamic_slice_in_dim(key_piece, offset, block_width, 1),
            lax.dynamic_slice_in_dim(value_piece, offset, block_width, 1),
            lax.dynamic_slice_in_dim(places, offset, block_width, 0),
            lax.dynamic_slice_in_dim(doc_list, offset, block_width, 0),
            query_heads,
            query_place,
            query_doc,
        )

    return lax.fori_loop(0, rounds, one_round, running)


def normalize(running, row_count):
    row_top, row_total, row_accum = running
    return (row_accum / row_total[:, :, None]).astype(jnp.bfloat16).reshape(row_count, -1)


def shards(queries, key_heads, value_heads, out_weight, block_order, doc_ids):
    row_count = queries.shape[0]
    head_count = queries.shape[1] // HD
    group_size = lax.axis_size("head") // KVH
    lane_index = lax.axis_index("head")
    kv_start = lane_index // group_size * HD
    key_part = lax.dynamic_slice_in_dim(key_heads, kv_start, HD, 0)
    value_part = lax.dynamic_slice_in_dim(value_heads, kv_start, HD, 0)
    ctx_index = lax.axis_index("ctx")
    own_rows = ctx_index * row_count + jnp.arange(row_count, dtype=jnp.int32)
    query_place, query_doc = locate(own_rows, block_order, doc_ids)
    query_heads = queries.reshape(row_count, head_count, HD)
    running = attend_span(
        (
            jnp.full((row_count, head_count), floor_score, jnp.float32),
            jnp.zeros((row_count, head_count), jnp.float32),
            jnp.zeros((row_count, head_count, HD), jnp.float32),
        ),
        lax.all_gather(key_part, "ctx", axis=1, tiled=True),
        lax.all_gather(value_part, "ctx", axis=1, tiled=True),
        query_heads,
        query_place,
        query_doc,
        block_order,
        doc_ids,
    )
    context = normalize(running, row_count)
    partial_sum = jnp.dot(context, out_weight, preferred_element_type=jnp.float32)
    return lax.psum_scatter(
        partial_sum.astype(jnp.bfloat16), "head", scatter_dimension=1, tiled=True
    )


def solution(mesh):
    placed = (P("ctx", "head"), P(None, "ctx"), P(None, "ctx"), P("head", None), P(), P())
    return jax.shard_map(
        shards, mesh=mesh, in_specs=placed, out_specs=P("ctx", "head"), check_vma=False
    )
```

profile of v0, /device:TPU:0, one launch (start us, length us, event | category | flops | bytes accessed | tf_op | source)
XLA Modules:
  0.0 472.5 jit_solution(731710215248140285)
XLA Ops:
  6.5 0.0 copy-start
  6.5 0.0 copy-start.2
  6.5 0.0 all-gather.3.cloned.1.call-start
  6.5 1.6 copy-done
  8.1 0.8 copy.20
  9.0 0.0 all-gather.3.cloned.1.call-update
  9.0 0.0 all-gather.5.cloned.1.call-start
  9.0 1.7 constant_dynamic-slice_fusion.1
  10.7 0.0 all-gather.5.cloned.1.call-update
  10.8 0.0 reduce-scatter.2.cloned.1.call-start
  10.8 0.7 select_reduce_fusion.1
  11.6 0.8 select_reduce_fusion
  12.4 5.8 %gather_fusion.1 = s32[1024]{0:T(1024)S(1)} fusion(s32[4096]{0:T(1024)} %param.13, s32[1024]{0:T(1024)S(1)} %broadcast_clamp_fusion.1), kind=kCustom, calls=%fused_computation.1 | custom fusion | bytes 12288 | tf_op jit(solution)/shard_map/jit(_take)/gather | solution.py:19
  18.3 0.0 copy-done.2
  18.3 23.0 %gather_fusion = s32[4096]{0:T(1024)S(1)} fusion(s32[4096]{0:T(1024)S(1)} %copy-done.2, s32[4096]{0:T(1024)S(1)} %broadcast_clamp_fusion), kind=kCustom, calls=%fused_computation | custom fusion | bytes 49152 | tf_op jit(solution)/shard_map/jit(_take)/gather | solution.py:19
  41.3 2.9 copy.16
  44.2 2.4 copy.17
  46.6 0.0 all-gather.3.cloned.1.call-done
  46.6 20.5 %all-gather.5.cloned.1.call-done = bf16[128,4096]{1,0:T(8,128)(2,1)} async-done(((bf16[128,1024]{1,0:T(8,128)(2,1)}), bf16[128,4096]{1,0:T(8,128)(2,1)}) %all-gather.5.cloned.1.call-update) | async-done | bytes 1048592 | tf_op jit(solution)/shard_map/all_gather | solution.py:92
  67.1 196.0 %while.18 = (s32[]{:T(128)}, f32[1024,8]{0,1:T(8,128)S(1)}, f32[1024,8]{0,1:T(8,128)S(1)}, f32[1024,8,128]{2,0,1:T(8,128)}, s32[4096]{0:T(1024)S(1)}, /*index=5*...) while((s32[]{:T(128)}, f32[1024,8]{0,1:T(8,128)S(1)}, ...), condition=%wide.region_5.6_spmd.clone, body=%wide.region_2.5_spmd.clone.sunk | while | flops 4410351616 | bytes 116424928 | solution.py:65
  67.1 1.2 compare_and_fusion.2
  68.2 14.9 %fusion.51 = (f32[1024,8]{0,1:T(8,128)S(1)}, f32[1024,1024,8]{1,0,2:T(8,128)}) fusion(pred[1024,1024]{0,1:T(8,128)(4,1)S(1)} %compare_and_fusion.2, bf16[1024,8,128]{2,0,1:T(8,128)(2,1)} %get-tuple-element.394, bf16[128,4096]{0,1:T(8,128)(2,1)} %get-tuple-element.393, s32[]{:T(128)S(6)} %select_n.212), kind=kOutput, calls=%fused_computation.4.clone.1 | convolution fusion | flops 2172641280 | bytes 36995076 | tf_op jit(solution)/shard_map/while/body/eval_jaxpr/thd,dk->thk/dot_general | solution.py:29
  83.1 14.7 %fusion.52 = f32[1024,8]{0,1:T(8,128)S(1)} fusion(f32[1024,1024,8]{1,0,2:T(8,128)} %get-tuple-element.352, f32[1024,8]{0,1:T(8,128)S(1)} %select_maximum_fusion.2, pred[1024,1024]{0,1:T(8,128)(4,1)S(1)} %compare_and_fusion.2), kind=kLoop, calls=%fused_computation.6.clone.1 | loop fusion | flops 41934848 | bytes 34668544 | tf_op jit(solution)/shard_map/while/body/eval_jaxpr/reduce_sum | solution.py:36
  97.9 17.4 %fusion.54 = f32[1024,8,128]{2,0,1:T(8,128)} fusion(f32[1024,8,128]{2,0,1:T(8,128)} %get-tuple-element.373, f32[1024,8]{0,1:T(8,128)S(1)} %get-tuple-element.354, pred[]{:T(512)S(6)} %compare.25, f32[1024,1024,8]{1,0,2:T(8,128)} %get-tuple-element.352, f32[1024,8]{0,1:T(8,128)S(1)} %select_maximum_fusion.2, ...), kind=kOutput, calls=%fused_computation.10.clone.1 | convolution fusion | flops 2192572416 | bytes 43319300 | tf_op jit(solution)/shard_map/while/body/eval_jaxpr/thk,dk->thd/dot_general | solution.py:37
  115.4 1.2 compare_and_fusion.2
  116.6 14.9 %fusion.51 = (f32[1024,8]{0,1:T(8,128)S(1)}, f32[1024,1024,8]{1,0,2:T(8,128)}) fusion(pred[1024,1024]{0,1:T(8,128)(4,1)S(1)} %compare_and_fusion.2, bf16[1024,8,128]{2,0,1:T(8,128)(2,1)} %get-tuple-element.394, bf16[128,4096]{0,1:T(8,128)(2,1)} %get-tuple-element.393, s32[]{:T(128)S(6)} %select_n.212), kind=kOutput, calls=%fused_computation.4.clone.1 | convolution fusion | flops 2172641280 | bytes 36995076 | tf_op jit(solution)/shard_map/while/body/eval_jaxpr/thd,dk->thk/dot_general | solution.py:29
  131.4 14.7 %fusion.52 = f32[1024,8]{0,1:T(8,128)S(1)} fusion(f32[1024,1024,8]{1,0,2:T(8,128)} %get-tuple-element.352, f32[1024,8]{0,1:T(8,128)S(1)} %select_maximum_fusion.2, pred[1024,1024]{0,1:T(8,128)(4,1)S(1)} %compare_and_fusion.2), kind=kLoop, calls=%fused_computation.6.clone.1 | loop fusion | flops 41934848 | bytes 34668544 | tf_op jit(solution)/shard_map/while/body/eval_jaxpr/reduce_sum | solution.py:36
  146.2 18.4 %fusion.54 = f32[1024,8,128]{2,0,1:T(8,128)} fusion(f32[1024,8,128]{2,0,1:T(8,128)} %get-tuple-element.373, f32[1024,8]{0,1:T(8,128)S(1)} %get-tuple-element.354, pred[]{:T(512)S(6)} %compare.25, f32[1024,1024,8]{1,0,2:T(8,128)} %get-tuple-element.352, f32[1024,8]{0,1:T(8,128)S(1)} %select_maximum_fusion.2, ...), kind=kOutput, calls=%fused_computation.10.clone.1 | convolution fusion | flops 2192572416 | bytes 43319300 | tf_op jit(solution)/shard_map/while/body/eval_jaxpr/thk,dk->thd/dot_general | solution.py:37
  164.6 1.2 compare_and_fusion.2
  165.8 14.9 %fusion.51 = (f32[1024,8]{0,1:T(8,128)S(1)}, f32[1024,1024,8]{1,0,2:T(8,128)}) fusion(pred[1024,1024]{0,1:T(8,128)(4,1)S(1)} %compare_and_fusion.2, bf16[1024,8,128]{2,0,1:T(8,128)(2,1)} %get-tuple-element.394, bf16[128,4096]{0,1:T(8,128)(2,1)} %get-tuple-element.393, s32[]{:T(128)S(6)} %select_n.212), kind=kOutput, calls=%fused_computation.4.clone.1 | convolution fusion | flops 2172641280 | bytes 36995076 | tf_op jit(solution)/shard_map/while/body/eval_jaxpr/thd,dk->thk/dot_general | solution.py:29
  180.7 14.7 %fusion.52 = f32[1024,8]{0,1:T(8,128)S(1)} fusion(f32[1024,1024,8]{1,0,2:T(8,128)} %get-tuple-element.352, f32[1024,8]{0,1:T(8,128)S(1)} %select_maximum_fusion.2, pred[1024,1024]{0,1:T(8,128)(4,1)S(1)} %compare_and_fusion.2), kind=kLoop, calls=%fused_computation.6.clone.1 | loop fusion | flops 41934848 | bytes 34668544 | tf_op jit(solution)/shard_map/while/body/eval_jaxpr/reduce_sum | solution.py:36
  195.4 18.4 %fusion.54 = f32[1024,8,128]{2,0,1:T(8,128)} fusion(f32[1024,8,128]{2,0,1:T(8,128)} %get-tuple-element.373, f32[1024,8]{0,1:T(8,128)S(1)} %get-tuple-element.354, pred[]{:T(512)S(6)} %compare.25, f32[1024,1024,8]{1,0,2:T(8,128)} %get-tuple-element.352, f32[1024,8]{0,1:T(8,128)S(1)} %select_maximum_fusion.2, ...), kind=kOutput, calls=%fused_computation.10.clone.1 | convolution fusion | flops 2192572416 | bytes 43319300 | tf_op jit(solution)/shard_map/while/body/eval_jaxpr/thk,dk->thd/dot_general | solution.py:37
  213.8 1.2 compare_and_fusion.2
  215.0 14.9 %fusion.51 = (f32[1024,8]{0,1:T(8,128)S(1)}, f32[1024,1024,8]{1,0,2:T(8,128)}) fusion(pred[1024,1024]{0,1:T(8,128)(4,1)S(1)} %compare_and_fusion.2, bf16[1024,8,128]{2,0,1:T(8,128)(2,1)} %get-tuple-element.394, bf16[128,4096]{0,1:T(8,128)(2,1)} %get-tuple-element.393, s32[]{:T(128)S(6)} %select_n.212), kind=kOutput, calls=%fused_computation.4.clone.1 | convolution fusion | flops 2172641280 | bytes 36995076 | tf_op jit(solution)/shard_map/while/body/eval_jaxpr/thd,dk->thk/dot_general | solution.py:29
  229.9 14.7 %fusion.52 = f32[1024,8]{0,1:T(8,128)S(1)} fusion(f32[1024,1024,8]{1,0,2:T(8,128)} %get-tuple-element.352, f32[1024,8]{0,1:T(8,128)S(1)} %select_maximum_fusion.2, pred[1024,1024]{0,1:T(8,128)(4,1)S(1)} %compare_and_fusion.2), kind=kLoop, calls=%fused_computation.6.clone.1 | loop fusion | flops 41934848 | bytes 34668544 | tf_op jit(solution)/shard_map/while/body/eval_jaxpr/reduce_sum | solution.py:36
  244.6 18.4 %fusion.54 = f32[1024,8,128]{2,0,1:T(8,128)} fusion(f32[1024,8,128]{2,0,1:T(8,128)} %get-tuple-element.373, f32[1024,8]{0,1:T(8,128)S(1)} %get-tuple-element.354, pred[]{:T(512)S(6)} %compare.25, f32[1024,1024,8]{1,0,2:T(8,128)} %get-tuple-element.352, f32[1024,8]{0,1:T(8,128)S(1)} %select_maximum_fusion.2, ...), kind=kOutput, calls=%fused_computation.10.clone.1 | convolution fusion | flops 2192572416 | bytes 43319300 | tf_op jit(solution)/shard_map/while/body/eval_jaxpr/thk,dk->thd/dot_general | solution.py:37
  263.0 5.5 %copy.18 = f32[1024,8,128]{0,2,1:T(8,128)} copy(f32[1024,8,128]{2,0,1:T(8,128)} %get-tuple-element.190) | data formatting | bytes 8388608 | tf_op jit(solution)/shard_map/while | solution.py:65
  268.6 2.8 divide_convert_fusion
  271.4 26.2 %convolution_convert_fusion = bf16[1024,8192]{1,0:T(8,128)(2,1)} fusion(bf16[1024,1024]{0,1:T(8,128)(2,1)S(1)} %bitcast.43, bf16[1024,8192]{1,0:T(8,128)(2,1)} %param.11), kind=kOutput, calls=%fused_computation.26 | convolution fusion | flops 17188257792 | bytes 35651584 | tf_op jit(solution)/shard_map/dot_general | solution.py:100
  297.5 0.0 copy-start.1
  297.5 0.0 reduce-scatter.2.cloned.1.call-update
  297.6 168.4 %reduce-scatter.2.cloned.1.call-done = bf16[1024,1024]{1,0:T(8,128)(2,1)} async-done(((bf16[1024,8192]{1,0:T(8,128)(2,1)}), bf16[1024,1024]{1,0:T(8,128)(2,1)}) %reduce-scatter.2.cloned.1.call-update) | async-done | bytes 2097168 | tf_op jit(solution)/shard_map/reduce_scatter | solution.py:101
  466.0 0.0 copy-done.1
  (34 shorter events, 0.3 us)
Async XLA Ops:
  6.5 1.6 copy-start
  6.5 11.7 %copy-start.2 = (s32[4096]{0:T(1024)S(1)}, s32[4096]{0:T(1024)}, u32[]{:S(2)}) copy-start(s32[4096]{0:T(1024)} %param.13) | copy-start | bytes 49156
  6.5 40.1 %all-gather.3.cloned.1.call-start = ((), (), s32[]{:S(2)}) async-start(), calls=%async_computation.1 | async-start | bytes 1310720 | tf_op jit(solution)/shard_map/all_gather | solution.py:91
  9.0 58.1 %all-gather.5.cloned.1.call-start = ((), (), s32[]{:S(2)}) async-start(), calls=%async_computation.2 | async-start | bytes 1310720 | tf_op jit(solution)/shard_map/all_gather | solution.py:92
  10.8 455.2 %reduce-scatter.2.cloned.1.call-start = ((), (), s32[]{:S(2)}) async-start(), calls=%async_computation.3 | async-start | bytes 18874368 | tf_op jit(solution)/shard_map/reduce_scatter | solution.py:101
  297.5 168.4 %copy-start.1 = (bf16[1024,1024]{1,0:T(8,128)(2,1)S(1)}, bf16[1024,1024]{1,0:T(8,128)(2,1)}, u32[]{:S(2)}) copy-start(bf16[1024,1024]{1,0:T(8,128)(2,1)} %param.9) | copy-start | bytes 6291460
Sparse Core Ops, SparseCore 0:
  9.2 29.3 all-gather.2
  40.4 26.6 all-gather.4
  297.7 168.2 reduce-scatter.1
where the time goes:
time: 474 us; the launch traced here: 472 us
  waiting for transfers between devices  189 us (40%)
  matrix products  158 us (33%)
  other arithmetic  68.1 us (14%)
  local copies, waits for them, and re-layouts  43.7 us (9%)
  between operations  13.3 us (3%)
    reduce_scatter x1, waiting for transfers between devices, shards(): lax.psum_scatter(partial_sum.astype(jnp.bfloat16), 'head', scatter_dimens...  168 us
    dot_general x4, matrix products, attend_block(): jnp.einsum('thk,dk->thd', weights.astype(jnp.bfloat16), value_block, pref...  72.6 us
    dot_general x4, matrix products, attend_block(): jnp.einsum('thd,dk->thk', query_heads, key_block, preferred_element_type=...  59.5 us
    reduce_sum x4, other arithmetic, attend_block(): row_total = row_total * factor + jnp.sum(weights, axis=2)  58.8 us
    gather x2, local copies, waits for them, and re-layouts, locate(): return (places, jnp.take(doc_ids, places))  28.8 us
    dot_general x1, matrix products, shards(): jnp.dot(context, out_weight, preferred_element_type=jnp.float32)  26.2 us
    all_gather x1, waiting for transfers between devices, shards(): lax.all_gather(value_part, 'ctx', axis=1, tiled=True)  20.5 us
  transfers between devices with their start and end apart: 3, of which 2 were waited for; matrix products, arithmetic and copies ran while one was open for 8% of the time, Pallas kernels for 0%

commit v1 on v0

--- a/solution.py
+++ b/solution.py
@@ -6,6 +6,18 @@
 KVH = 8
 HD = 128
 floor_score = -1e30
+
+
+def collect(x, axis, dim):
+    ways, here, step = (lax.axis_size(axis), lax.axis_index(axis), x.shape[dim])
+    line, have = (x, 1)
+    while have < ways:
+        line = jnp.concatenate(
+            [line, lax.ppermute(line, axis, [(d, (d - have) % ways) for d in range(ways)])],
+            axis=dim,
+        )
+        have = 2 * have
+    return jnp.roll(line, here * step, axis=dim)
 
 
 def locate(row_ids, block_order, doc_ids):
@@ -89,7 +101,7 @@
             jnp.zeros((row_count, head_count, HD), jnp.float32),
         ),
         lax.all_gather(key_part, "ctx", axis=1, tiled=True),
-        lax.all_gather(value_part, "ctx", axis=1, tiled=True),
+        collect(value_part, "ctx", 1),
         query_heads,
         query_place,
         query_doc,

time: 474 us -> 465 us (0.981)
  waiting for transfers between devices: 189 us -> 169 us
  local copies, waits for them, and re-layouts: 43.7 us -> 49.5 us
    all_gather x1 -> x0, waiting for transfers between devices: 20.5 us -> none  [shards(): lax.all_gather(value_part, 'ctx', axis=1, tiled=True)]
    unnamed x9 -> x14, local copies, waits for them, and re-layouts: 7.66 us -> 12.5 us
  transfers between devices with their start and end apart: 3 -> 4, of which waited for: 2 -> 1; matrix products, arithmetic and copies ran while one was open for 8% -> 9% of each run, Pallas kernels for 0% -> 0%
where the time goes in v1:
time: 465 us; the launch traced here: 464 us
  waiting for transfers between devices  169 us (36%)
  matrix products  158 us (34%)
  other arithmetic  68.9 us (15%)
  local copies, waits for them, and re-layouts  49.5 us (11%)
  between operations  13.6 us (3%)
    reduce_scatter x1, waiting for transfers between devices, shards(): lax.psum_scatter(partial_sum.astype(jnp.bfloat16), 'head', scatter_dimens...  169 us
    dot_general x4, matrix products, attend_block(): jnp.einsum('thk,dk->thd', weights.astype(jnp.bfloat16), value_block, pref...  72.3 us
    dot_general x4, matrix products, attend_block(): jnp.einsum('thd,dk->thk', query_heads, key_block, preferred_element_type=...  59.5 us
    reduce_sum x4, other arithmetic, attend_block(): row_total = row_total * factor + jnp.sum(weights, axis=2)  58.8 us
    gather x2, local copies, waits for them, and re-layouts, locate(): return (places, jnp.take(doc_ids, places))  29.2 us
    dot_general x1, matrix products, shards(): jnp.dot(context, out_weight, preferred_element_type=jnp.float32)  26.2 us
    unnamed x14, local copies, waits for them, and re-layouts  12.5 us
  transfers between devices with their start and end apart: 4, of which 1 were waited for; matrix products, arithmetic and copies ran while one was open for 9% of the time, Pallas kernels for 0%

profile of v1, /device:TPU:0, one launch (start us, length us, event | category | flops | bytes accessed | tf_op | source)
XLA Modules:
  0.0 463.9 jit_solution(16658940914059973559)
XLA Ops:
  6.5 0.0 copy-start
  6.5 0.0 copy-start.2
  6.5 0.0 all-gather.2.cloned.1.call-start
  6.5 1.6 copy-done
  8.1 0.8 copy.20
  9.0 0.0 all-gather.2.cloned.1.call-update
  9.0 0.0 reduce-scatter.2.cloned.1.call-start
  9.1 1.8 constant_dynamic-update-slice_fusion.5
  10.8 3.9 collective-permute-start
  14.7 0.7 select_reduce_fusion.1
  15.5 0.8 select_reduce_fusion
  16.4 0.0 copy-done.2
  16.4 6.2 %gather_fusion.1 = s32[1024]{0:T(1024)S(1)} fusion(s32[4096]{0:T(1024)S(1)} %copy-done.2, s32[1024]{0:T(1024)S(1)} %broadcast_clamp_fusion.1), kind=kCustom, calls=%fused_computation.1 | custom fusion | bytes 12288 | tf_op jit(solution)/shard_map/jit(_take)/gather | solution.py:31
  22.5 0.0 collective-permute-done
  22.6 0.8 pad_maximum_fusion
  23.4 0.5 collective-permute-start.1
  24.0 23.0 %gather_fusion = s32[4096]{0:T(1024)S(1)} fusion(s32[4096]{0:T(1024)S(1)} %copy-done.2, s32[4096]{0:T(1024)S(1)} %broadcast_clamp_fusion), kind=kCustom, calls=%fused_computation | custom fusion | bytes 49152 | tf_op jit(solution)/shard_map/jit(_take)/gather | solution.py:31
  47.0 2.9 copy.16
  49.9 2.4 copy.17
  52.3 0.7 constant_dynamic-update-slice_fusion.4
  53.0 0.0 collective-permute-done.1
  53.0 0.9 constant_dynamic-update-slice_fusion.3
  53.9 0.7 constant_dynamic-update-slice_fusion.2
  54.6 0.8 constant_dynamic-update-slice_fusion.1
  55.3 0.9 constant_dynamic-update-slice_fusion
  56.2 1.3 constant_dynamic-slice_fusion.2
  57.6 0.0 all-gather.2.cloned.1.call-done
  57.6 195.7 %while.18 = (s32[]{:T(128)}, f32[1024,8]{0,1:T(8,128)S(1)}, f32[1024,8]{0,1:T(8,128)S(1)}, f32[1024,8,128]{2,0,1:T(8,128)}, s32[4096]{0:T(1024)S(1)}, /*index=5*...) while((s32[]{:T(128)}, f32[1024,8]{0,1:T(8,128)S(1)}, ...), condition=%wide.region_5.6_spmd.clone, body=%wide.region_2.5_spmd.clone.sunk | while | flops 4410351616 | bytes 116424928 | solution.py:77
  57.6 1.2 compare_and_fusion.2
  58.8 14.9 %fusion.51 = (f32[1024,8]{0,1:T(8,128)S(1)}, f32[1024,1024,8]{1,0,2:T(8,128)}) fusion(pred[1024,1024]{0,1:T(8,128)(4,1)S(1)} %compare_and_fusion.2, bf16[1024,8,128]{2,0,1:T(8,128)(2,1)} %get-tuple-element.396, bf16[128,4096]{0,1:T(8,128)(2,1)} %get-tuple-element.395, s32[]{:T(128)S(6)} %select_n.226), kind=kOutput, calls=%fused_computation.4.clone.1 | convolution fusion | flops 2172641280 | bytes 36995076 | tf_op jit(solution)/shard_map/while/body/eval_jaxpr/thd,dk->thk/dot_general | solution.py:41
  73.7 14.7 %fusion.52 = f32[1024,8]{0,1:T(8,128)S(1)} fusion(f32[1024,1024,8]{1,0,2:T(8,128)} %get-tuple-element.354, f32[1024,8]{0,1:T(8,128)S(1)} %select_maximum_fusion.2, pred[1024,1024]{0,1:T(8,128)(4,1)S(1)} %compare_and_fusion.2), kind=kLoop, calls=%fused_computation.6.clone.1 | loop fusion | flops 41934848 | bytes 34668544 | tf_op jit(solution)/shard_map/while/body/eval_jaxpr/reduce_sum | solution.py:48
  88.5 17.4 %fusion.54 = f32[1024,8,128]{2,0,1:T(8,128)} fusion(f32[1024,8,128]{2,0,1:T(8,128)} %get-tuple-element.375, f32[1024,8]{0,1:T(8,128)S(1)} %get-tuple-element.356, pred[]{:T(512)S(6)} %compare.26, f32[1024,1024,8]{1,0,2:T(8,128)} %get-tuple-element.354, f32[1024,8]{0,1:T(8,128)S(1)} %select_maximum_fusion.2, ...), kind=kOutput, calls=%fused_computation.10.clone.1 | convolution fusion | flops 2192572416 | bytes 43319300 | tf_op jit(solution)/shard_map/while/body/eval_jaxpr/thk,dk->thd/dot_general | solution.py:49
  105.9 1.2 compare_and_fusion.2
  107.1 14.9 %fusion.51 = (f32[1024,8]{0,1:T(8,128)S(1)}, f32[1024,1024,8]{1,0,2:T(8,128)}) fusion(pred[1024,1024]{0,1:T(8,128)(4,1)S(1)} %compare_and_fusion.2, bf16[1024,8,128]{2,0,1:T(8,128)(2,1)} %get-tuple-element.396, bf16[128,4096]{0,1:T(8,128)(2,1)} %get-tuple-element.395, s32[]{:T(128)S(6)} %select_n.226), kind=kOutput, calls=%fused_computation.4.clone.1 | convolution fusion | flops 2172641280 | bytes 36995076 | tf_op jit(solution)/shard_map/while/body/eval_jaxpr/thd,dk->thk/dot_general | solution.py:41
  122.0 14.7 %fusion.52 = f32[1024,8]{0,1:T(8,128)S(1)} fusion(f32[1024,1024,8]{1,0,2:T(8,128)} %get-tuple-element.354, f32[1024,8]{0,1:T(8,128)S(1)} %select_maximum_fusion.2, pred[1024,1024]{0,1:T(8,128)(4,1)S(1)} %compare_and_fusion.2), kind=kLoop, calls=%fused_computation.6.clone.1 | loop fusion | flops 41934848 | bytes 34668544 | tf_op jit(solution)/shard_map/while/body/eval_jaxpr/reduce_sum | solution.py:48
  136.7 18.3 %fusion.54 = f32[1024,8,128]{2,0,1:T(8,128)} fusion(f32[1024,8,128]{2,0,1:T(8,128)} %get-tuple-element.375, f32[1024,8]{0,1:T(8,128)S(1)} %get-tuple-element.356, pred[]{:T(512)S(6)} %compare.26, f32[1024,1024,8]{1,0,2:T(8,128)} %get-tuple-element.354, f32[1024,8]{0,1:T(8,128)S(1)} %select_maximum_fusion.2, ...), kind=kOutput, calls=%fused_computation.10.clone.1 | convolution fusion | flops 2192572416 | bytes 43319300 | tf_op jit(solution)/shard_map/while/body/eval_jaxpr/thk,dk->thd/dot_general | solution.py:49
  155.1 1.2 compare_and_fusion.2
  156.3 14.9 %fusion.51 = (f32[1024,8]{0,1:T(8,128)S(1)}, f32[1024,1024,8]{1,0,2:T(8,128)}) fusion(pred[1024,1024]{0,1:T(8,128)(4,1)S(1)} %compare_and_fusion.2, bf16[1024,8,128]{2,0,1:T(8,128)(2,1)} %get-tuple-element.396, bf16[128,4096]{0,1:T(8,128)(2,1)} %get-tuple-element.395, s32[]{:T(128)S(6)} %select_n.226), kind=kOutput, calls=%fused_computation.4.clone.1 | convolution fusion | flops 2172641280 | bytes 36995076 | tf_op jit(solution)/shard_map/while/body/eval_jaxpr/thd,dk->thk/dot_general | solution.py:41
  171.1 14.7 %fusion.52 = f32[1024,8]{0,1:T(8,128)S(1)} fusion(f32[1024,1024,8]{1,0,2:T(8,128)} %get-tuple-element.354, f32[1024,8]{0,1:T(8,128)S(1)} %select_maximum_fusion.2, pred[1024,1024]{0,1:T(8,128)(4,1)S(1)} %compare_and_fusion.2), kind=kLoop, calls=%fused_computation.6.clone.1 | loop fusion | flops 41934848 | bytes 34668544 | tf_op jit(solution)/shard_map/while/body/eval_jaxpr/reduce_sum | solution.py:48
  185.9 18.3 %fusion.54 = f32[1024,8,128]{2,0,1:T(8,128)} fusion(f32[1024,8,128]{2,0,1:T(8,128)} %get-tuple-element.375, f32[1024,8]{0,1:T(8,128)S(1)} %get-tuple-element.356, pred[]{:T(512)S(6)} %compare.26, f32[1024,1024,8]{1,0,2:T(8,128)} %get-tuple-element.354, f32[1024,8]{0,1:T(8,128)S(1)} %select_maximum_fusion.2, ...), kind=kOutput, calls=%fused_computation.10.clone.1 | convolution fusion | flops 2192572416 | bytes 43319300 | tf_op jit(solution)/shard_map/while/body/eval_jaxpr/thk,dk->thd/dot_general | solution.py:49
  204.2 1.2 compare_and_fusion.2
  205.4 14.9 %fusion.51 = (f32[1024,8]{0,1:T(8,128)S(1)}, f32[1024,1024,8]{1,0,2:T(8,128)}) fusion(pred[1024,1024]{0,1:T(8,128)(4,1)S(1)} %compare_and_fusion.2, bf16[1024,8,128]{2,0,1:T(8,128)(2,1)} %get-tuple-element.396, bf16[128,4096]{0,1:T(8,128)(2,1)} %get-tuple-element.395, s32[]{:T(128)S(6)} %select_n.226), kind=kOutput, calls=%fused_computation.4.clone.1 | convolution fusion | flops 2172641280 | bytes 36995076 | tf_op jit(solution)/shard_map/while/body/eval_jaxpr/thd,dk->thk/dot_general | solution.py:41
  220.3 14.7 %fusion.52 = f32[1024,8]{0,1:T(8,128)S(1)} fusion(f32[1024,1024,8]{1,0,2:T(8,128)} %get-tuple-element.354, f32[1024,8]{0,1:T(8,128)S(1)} %select_maximum_fusion.2, pred[1024,1024]{0,1:T(8,128)(4,1)S(1)} %compare_and_fusion.2), kind=kLoop, calls=%fused_computation.6.clone.1 | loop fusion | flops 41934848 | bytes 34668544 | tf_op jit(solution)/shard_map/while/body/eval_jaxpr/reduce_sum | solution.py:48
  235.0 18.3 %fusion.54 = f32[1024,8,128]{2,0,1:T(8,128)} fusion(f32[1024,8,128]{2,0,1:T(8,128)} %get-tuple-element.375, f32[1024,8]{0,1:T(8,128)S(1)} %get-tuple-element.356, pred[]{:T(512)S(6)} %compare.26, f32[1024,1024,8]{1,0,2:T(8,128)} %get-tuple-element.354, f32[1024,8]{0,1:T(8,128)S(1)} %select_maximum_fusion.2, ...), kind=kOutput, calls=%fused_computation.10.clone.1 | convolution fusion | flops 2192572416 | bytes 43319300 | tf_op jit(solution)/shard_map/while/body/eval_jaxpr/thk,dk->thd/dot_general | solution.py:49
  253.3 5.5 %copy.18 = f32[1024,8,128]{0,2,1:T(8,128)} copy(f32[1024,8,128]{2,0,1:T(8,128)} %get-tuple-element.190) | data formatting | bytes 8388608 | tf_op jit(solution)/shard_map/while | solution.py:77
  258.8 2.8 divide_convert_fusion
  261.6 26.2 %convolution_convert_fusion = bf16[1024,8192]{1,0:T(8,128)(2,1)} fusion(bf16[1024,1024]{0,1:T(8,128)(2,1)S(1)} %bitcast.43, bf16[1024,8192]{1,0:T(8,128)(2,1)} %param.11), kind=kOutput, calls=%fused_computation.26 | convolution fusion | flops 17188257792 | bytes 35651584 | tf_op jit(solution)/shard_map/dot_general | solution.py:112
  287.8 0.0 reduce-scatter.2.cloned.1.call-update
  287.8 0.0 copy-start.1
  287.9 169.2 %reduce-scatter.2.cloned.1.call-done = bf16[1024,1024]{1,0:T(8,128)(2,1)} async-done(((bf16[1024,8192]{1,0:T(8,128)(2,1)}), bf16[1024,1024]{1,0:T(8,128)(2,1)}) %reduce-scatter.2.cloned.1.call-update) | async-done | bytes 2097168 | tf_op jit(solution)/shard_map/reduce_scatter | solution.py:113
  457.0 0.0 copy-done.1
  (34 shorter events, 0.3 us)
Async XLA Ops:
  6.5 1.6 copy-start
  6.5 9.8 %copy-start.2 = (s32[4096]{0:T(1024)S(1)}, s32[4096]{0:T(1024)}, u32[]{:S(2)}) copy-start(s32[4096]{0:T(1024)} %param.13) | copy-start | bytes 49156
  6.5 51.0 %all-gather.2.cloned.1.call-start = ((), (), s32[]{:S(2)}) async-start(), calls=%async_computation.1 | async-start | bytes 1310720 | tf_op jit(solution)/shard_map/all_gather | solution.py:103
  9.0 448.0 %reduce-scatter.2.cloned.1.call-start = ((), (), s32[]{:S(2)}) async-start(), calls=%async_computation.2 | async-start | bytes 18874368 | tf_op jit(solution)/shard_map/reduce_scatter | solution.py:113
  10.8 11.7 %collective-permute-start = (bf16[128,1024]{1,0:T(8,128)(2,1)S(1)}, bf16[128,1024]{1,0:T(8,128)(2,1)S(1)}, u32[]{:S(2)}, u32[]{:S(2)}) collective-permute-start(bf16[128,1024]{1,0:T(8,128)(2,1)S(1)} %get-tuple-element.275), channel_id=1, source_target_pairs={{0,24},{8,0},{16,8},{24,16},{1,25},{9,1},{17,9},{25,17},{2,26},{10... | collective-permute-start | bytes 786440 | tf_op jit(solution)/shard_map/ppermute | solution.py:16
  23.4 29.6 %collective-permute-start.1 = (bf16[128,2048]{1,0:T(8,128)(2,1)}, bf16[128,2048]{1,0:T(8,128)(2,1)S(1)}, u32[]{:S(2)}, u32[]{:S(2)}) collective-permute-start(bf16[128,2048]{1,0:T(8,128)(2,1)} %pad_maximum_fusion), channel_id=1, source_target_pairs={{0,16},{8,24},{16,0},{24,8},{1,17},{9,25},{17,1},{25,9},{2,18},{10... | collective-permute-start | bytes 1572872 | tf_op jit(solution)/shard_map/ppermute | solution.py:16
  287.8 169.2 %copy-start.1 = (bf16[1024,1024]{1,0:T(8,128)(2,1)S(1)}, bf16[1024,1024]{1,0:T(8,128)(2,1)}, u32[]{:S(2)}) copy-start(bf16[1024,1024]{1,0:T(8,128)(2,1)} %param.9) | copy-start | bytes 6291460
Sparse Core Ops, SparseCore 0:
  9.2 33.6 all-gather.1
  288.0 169.0 reduce-scatter.1
